TPU v7x, 32 devices: a whole 2x2x4 slice. The times are simulated.
32 devices in a mesh: tok: 8 (over y, x, core), lat: 4 (over z).
Axes of the slice: x: 2, y: 2, z: 4, core: 2. Of those that a mesh axis runs over, the one named last changes fastest.
Arguments:
- captured: bfloat16 [1024, 16384], P(None, 'tok'), may hold values from -6 to 6
- enc_weight: bfloat16 [16384, 16384], P('tok', 'lat'), may hold values from -0.046875 to 0.046875
- enc_bias: float32 [16384], P('lat'), may hold values from -3 to 3
- dec_weight: bfloat16 [16384, 16384], P('lat', 'tok'), may hold values from -0.1875 to 0.1875
- dec_bias: float32 [16384], P('tok'), may hold values from -1.5 to 1.5
- block_ids: int32 [8, 4, 2], P(None, 'lat'), may hold values from 0 to 31, as said below
- block_counts: int32 [8, 4], P(None, 'lat'), may hold values from 1 to 2, as said below
Outputs:
- enc_grad: bfloat16 [16384, 16384], P('tok', 'lat')
- dec_grad: bfloat16 [16384, 16384], P('lat', 'tok')
Inputs may be any that keep to these rules, and one draw needn't show every extreme that they name: block_ids[b, s, k] numbers a latent block within latent shard s; the 2 entries of one token block and shard are distinct, and those with k >= block_counts[b, s] are inactive slots. block_counts[b, s] is how many leading slots of block_ids[b, s] are active; some entry equals 2 in every draw.
All inputs are finite; a program needn't handle non-finite values.
Results may differ from a plain program's by a relative error of at most 0.02.
Values may be sent and summed in bfloat16 or wider, within the bound.
A program may use at most 192 MiB of HBM per device.

v0:
```python
import jax
import jax.numpy as jnp
from jax import lax
from jax.sharding import PartitionSpec as P

TB = 128
LB = 128
KS = 2


SCALE_ERR = 0.0625
PENALTY = 0.05


def local(captured, enc_weight, enc_bias, dec_weight, dec_bias, block_ids, block_counts):
    features = captured.shape[1]
    lat_dev = enc_weight.shape[1]
    lat_blocks = lat_dev // LB
    all_blocks = captured.shape[0] // TB
    own_blocks = all_blocks // lax.axis_size("tok")
    first_block = lax.axis_index("tok") * own_blocks
    ids_all = block_ids.reshape(all_blocks, KS)
    counts_all = block_counts.reshape(all_blocks)
    enc_cube = enc_weight.reshape(features, lat_blocks, LB)
    dec_cube = dec_weight.reshape(lat_blocks, LB, features)
    acts_blocks = captured.reshape(all_blocks, TB, features)
    selector = (
        ids_all[:, :, None] == jnp.arange(lat_blocks, dtype=jnp.int32)[None, None, :]
    ).astype(jnp.float32)
    block_rows = acts_blocks
    chosen = ids_all
    weight_tiles = jnp.take(enc_cube, chosen, axis=1)
    pre_sum = lax.psum_scatter(
        jnp.einsum(
            "btf,fbkc->bktc", block_rows, weight_tiles, preferred_element_type=jnp.float32
        ).astype(jnp.bfloat16),
        "tok",
        scatter_dimension=0,
        tiled=True,
    ).astype(jnp.float32)
    own_ids = lax.dynamic_slice_in_dim(ids_all, first_block, own_blocks, 0)
    own_counts = lax.dynamic_slice_in_dim(counts_all, first_block, own_blocks, 0)
    bias_tiles = jnp.take(enc_bias.reshape(lat_blocks, LB), own_ids, axis=0)
    live_slots = (jnp.arange(KS, dtype=jnp.int32)[None, :] < own_counts[:, None]).astype(
        jnp.float32
    )
    pre_act = pre_sum + bias_tiles[:, :, None, :]
    codes_own = (jax.nn.softplus(pre_act) * live_slots[:, :, None, None]).astype(jnp.bfloat16)
    codes_all = lax.all_gather(codes_own, "tok", axis=0, tiled=True)
    dec_tiles = jnp.take(dec_cube, ids_all, axis=0)
    partial_value = jnp.einsum(
        "bktc,bkcf->btf", codes_all, dec_tiles, preferred_element_type=jnp.float32
    )
    partial_value = lax.optimization_barrier(partial_value.astype(jnp.bfloat16)).astype(jnp.float32)
    rebuilt = lax.psum(
        partial_value.reshape(all_blocks * TB, features).astype(jnp.bfloat16), "lat"
    ).astype(jnp.float32)
    err_grad = SCALE_ERR * (rebuilt + dec_bias[None, :] - captured.astype(jnp.float32))
    err_half = err_grad.astype(jnp.bfloat16).reshape(all_blocks, TB, features)
    tile_grads = jnp.einsum(
        "bktc,btf->bkcf", codes_all, err_half, preferred_element_type=jnp.float32
    )
    dec_total = jnp.einsum("bkj,bkcf->jcf", selector, tile_grads, precision=lax.Precision.HIGHEST)
    dec_grad = dec_total.reshape(lat_dev, features).astype(jnp.bfloat16)
    weight_tiles = dec_tiles
    dcode_all = lax.psum(
        jnp.einsum(
            "btf,bkcf->bktc", err_half, weight_tiles, preferred_element_type=jnp.float32
        ).astype(jnp.bfloat16),
        "tok",
    ).astype(jnp.float32)
    dpre_all = ((dcode_all + PENALTY) * (1.0 - jnp.exp(-codes_all.astype(jnp.float32)))).astype(
        jnp.bfloat16
    )
    block_rows = acts_blocks
    chosen = selector
    products = jnp.einsum(
        "btf,bktc->bkfc", block_rows, dpre_all, preferred_element_type=jnp.float32
    )
    enc_total = jnp.einsum("bkj,bkfc->fjc", chosen, products, precision=lax.Precision.HIGHEST)
    enc_grad = enc_total.reshape(features, lat_dev).astype(jnp.bfloat16)
    return (enc_grad, dec_grad)


def solution(mesh):
    in_specs = (
        P(None, "tok"),
        P("tok", "lat"),
        P("lat"),
        P("lat", "tok"),
        P("tok"),
        P(None, "lat", None),
        P(None, "lat"),
    )
    out_specs = (P("tok", "lat"), P("lat", "tok"))
    return jax.shard_map(local, mesh=mesh, in_specs=in_specs, out_specs=out_specs, check_vma=False)
```

profile of v0, /device:TPU:0, one launch (start us, length us, event | category | flops | bytes accessed | tf_op | source)
XLA Modules:
  0.0 444.1 jit_solution(18071114401110262952)
XLA Ops:
  7.2 0.0 copy-start
  7.2 0.0 reduce-scatter.2.cloned.1.call-start
  7.2 0.7 compare_and_fusion.1
  7.9 0.7 compare_select_fusion.1
  8.6 0.1 copy.30
  8.7 0.1 copy.31
  8.8 0.1 reshape.177
  8.9 22.4 %copy.33 = bf16[2048,4096]{0,1:T(8,128)(2,1)} copy(bf16[2048,4096]{1,0:T(8,128)(2,1)} %param.8) | data formatting | bytes 33554432 | tf_op args[1]
  31.3 22.4 %copy.34 = bf16[2048,32,128]{2,0,1:T(8,128)(2,1)} copy(bf16[2048,32,128]{0,2,1:T(8,128)(2,1)} %bitcast.68) | data formatting | bytes 33554432 | tf_op jit(solution)/shard_map/reshape | solution.py:24
  53.7 10.7 %gather_fusion.1 = bf16[16,2048,128]{2,1,0:T(8,128)(2,1)} fusion(bf16[2048,32,128]{2,0,1:T(8,128)(2,1)} %copy.34, s32[1024]{0:T(1024)S(1)} %pad_clamp_fusion.1), kind=kCustom, calls=%fused_computation.1 | custom fusion | bytes 16777280 | tf_op jit(solution)/shard_map/jit(_take)/gather | solution.py:32
  64.4 11.4 %copy.35 = bf16[8,2,2048,128]{2,3,1,0:T(8,128)(2,1)} copy(bf16[8,2,2048,128]{3,2,1,0:T(8,128)(2,1)} %bitcast.69) | data formatting | bytes 16777216 | tf_op jit(solution)/shard_map/jit(_take)/gather | solution.py:32
  75.8 0.0 copy-start.3
  75.8 0.0 copy-start.5
  75.8 7.8 %fusion.14 = bf16[8,2,128,128]{2,3,1,0:T(8,128)(2,1)} fusion(bf16[8,128,2048,1]{2,1,3,0:T(8,128)(2,1)} %bitcast.72, bf16[8,2,2048,128]{2,3,1,0:T(8,128)(2,1)} %copy.35, pred[8,2]{1,0:T(8,128)(4,1)S(1)} %copy.30), kind=kOutput, calls=%fused_computation.22 | convolution fusion | flops 1078198272 | bytes 13107216 | tf_op jit(solution)/shard_map/btf,fbkc->bktc/dot_general | solution.py:34
  83.6 0.0 reduce-scatter.2.cloned.1.call-update
  83.6 0.0 all-reduce.3.cloned.1.call-start
  83.6 0.0 copy-done.3
  83.6 0.2 dynamic-slice_reduce_fusion
  83.8 0.0 copy-done.5
  83.8 0.6 constant_dynamic-slice_fusion
  84.4 10.7 %gather_fusion = bf16[16,128,2048]{2,1,0:T(8,128)(2,1)} fusion(bf16[32,128,2048]{2,1,0:T(8,128)(2,1)} %bitcast.78, s32[1024]{0:T(1024)S(1)} %pad_clamp_fusion.1), kind=kCustom, calls=%fused_computation | custom fusion | bytes 16777280 | tf_op jit(solution)/shard_map/jit(_take)/gather | solution.py:50
  95.1 0.0 copy-done
  95.2 0.6 gather_fusion.2
  95.7 0.6 compare_convert_fusion
  96.4 0.1 broadcast_select_fusion.9
  96.5 24.2 %reduce-scatter.2.cloned.1.call-done = bf16[1,2,128,128]{2,3,1,0:T(8,128)(2,1)} async-done(((bf16[8,2,128,128]{2,3,1,0:T(8,128)(2,1)}), bf16[1,2,128,128]{2,3,1,0:T(8,128)(2,1)}) %reduce-scatter.2.cloned.1.call-update) | async-done | bytes 65552 | tf_op jit(solution)/shard_map/reduce_scatter | solution.py:33
  120.6 1.0 fusion.21
  121.6 0.1 copy.36
  121.7 9.8 %all_gather.3 = bf16[8,2,128,128]{3,2,1,0:T(8,128)(2,1)S(1)} all-gather(bf16[1,2,128,128]{3,2,1,0:T(8,128)(2,1)S(1)} %copy.36), channel_id=1, replica_groups=mesh['tok'=8,'lat'=4] {'tok'}, dimensions={0}, use_global_device_ids=true | all-gather | bytes 589824 | tf_op jit(solution)/shard_map/all_gather | solution.py:49
  131.6 0.0 copy-start.4
  131.6 7.0 %bitcast_convert_fusion.2 = bf16[8,128,2048]{2,1,0:T(8,128)(2,1)} fusion(bf16[8,2,128,128]{3,2,1,0:T(8,128)(2,1)S(1)} %all_gather.3, bf16[8,2,128,2048]{3,2,1,0:T(8,128)(2,1)} %bitcast.76, pred[8,2]{1,0:T(8,128)(4,1)S(1)} %copy.30), kind=kOutput, calls=%fused_computation.7 | convolution fusion | flops 1080033280 | bytes 13107216 | tf_op jit(solution)/shard_map/bktc,bkcf->btf/dot_general | solution.py:51
  138.5 0.0 all-reduce.3.cloned.1.call-update
  138.5 0.2 all-reduce.5.cloned.1.call-start
  138.8 0.3 copy.37
  139.1 154.6 %all-reduce.3.cloned.1.call-done = bf16[1024,2048]{1,0:T(8,128)(2,1)} async-done(((bf16[1024,2048]{1,0:T(8,128)(2,1)}), bf16[1024,2048]{1,0:T(8,128)(2,1)}) %all-reduce.3.cloned.1.call-update) | async-done | bytes 4194320 | tf_op jit(solution)/shard_map/psum | solution.py:55
  293.7 0.0 copy-done.4
  293.7 5.5 %multiply_convert_fusion = bf16[1024,2048]{1,0:T(8,128)(2,1)S(1)} fusion(bf16[1024,2048]{1,0:T(8,128)(2,1)} %param.7, bf16[1024,2048]{1,0:T(8,128)(2,1)} %all-reduce.3.cloned.1.call-done, f32[2048]{0:T(1024)S(1)} %copy-done.4), kind=kLoop, calls=%fused_computation.11 | loop fusion | flops 12582912 | bytes 12591104 | tf_op jit(solution)/shard_map/convert_element_type | solution.py:59
  299.2 0.0 copy-start.2
  299.2 2.0 copy-done.2
  301.2 6.5 %fusion.17 = bf16[8,2,128,128]{2,3,1,0:T(8,128)(2,1)} fusion(bf16[8,128,2048,1]{2,1,3,0:T(8,128)(2,1)S(1)} %bitcast.74, bf16[8,2,128,2048]{3,2,1,0:T(8,128)(2,1)} %bitcast.77, pred[8,2]{1,0:T(8,128)(4,1)S(1)} %copy.30), kind=kOutput, calls=%fused_computation.23 | convolution fusion | flops 1078198272 | bytes 13107216 | tf_op jit(solution)/shard_map/btf,bkcf->bktc/dot_general | solution.py:67
  307.8 10.7 %fusion.33 = f32[8,2,128,2048]{3,2,1,0:T(8,128)} fusion(bf16[8,2,128,128]{3,2,1,0:T(8,128)(2,1)S(1)} %all_gather.3, bf16[8,128,2048,1]{2,1,3,0:T(8,128)(2,1)} %bitcast.75), kind=kOutput, calls=%fused_computation.52 | convolution fusion | flops 1073741824 | bytes 21495808 | tf_op jit(solution)/shard_map/bktc,btf->bkcf/dot_general | solution.py:60
  318.5 0.0 all-reduce.5.cloned.1.call-update
  318.5 26.5 %bitcast_convert_fusion = bf16[32,128,2048]{2,0,1:T(8,128)(2,1)S(1)} fusion(f32[8,2,128,2048]{3,2,1,0:T(8,128)} %fusion.33, s32[8,2]{0,1:T(2,128)S(1)} %bitcast.80), kind=kOutput, calls=%fused_computation.3 | convolution fusion | flops 1619001856 | bytes 33554496 | tf_op jit(solution)/shard_map/bkj,bkcf->jcf/dot_general | solution.py:63
  345.0 20.9 %copy.41 = bf16[32,128,2048]{2,1,0:T(8,128)(2,1)} copy(bf16[32,128,2048]{2,0,1:T(8,128)(2,1)S(1)} %bitcast_convert_fusion) | data formatting | bytes 33554432 | tf_op jit(solution)/shard_map/convert_element_type | solution.py:64
  366.0 6.4 %all-reduce.5.cloned.1.call-done = bf16[8,2,128,128]{2,3,1,0:T(8,128)(2,1)} async-done(((bf16[8,2,128,128]{2,3,1,0:T(8,128)(2,1)}), bf16[8,2,128,128]{2,3,1,0:T(8,128)(2,1)}) %all-reduce.5.cloned.1.call-update) | async-done | bytes 524304 | tf_op jit(solution)/shard_map/psum | solution.py:66
  372.4 10.9 %convolution_bitcast_fusion = f32[8,2,2048,128]{2,3,1,0:T(8,128)} fusion(bf16[8,128,2048,1]{2,1,3,0:T(8,128)(2,1)} %bitcast.73, bf16[8,2,128,128]{2,3,1,0:T(8,128)(2,1)S(1)} %copy.37, bf16[8,2,128,128]{2,3,1,0:T(8,128)(2,1)} %all-reduce.5.cloned.1.call-done), kind=kOutput, calls=%fused_computation.16 | convolution fusion | flops 1075576832 | bytes 22020096 | tf_op jit(solution)/shard_map/btf,bktc->bkfc/dot_general | solution.py:77
  383.3 17.8 %copy.38 = f32[8,2,2048,128]{3,0,1,2:T(8,128)} copy(f32[8,2,2048,128]{2,3,1,0:T(8,128)} %convolution_bitcast_fusion) | data formatting | bytes 33554432 | tf_op jit(solution)/shard_map/btf,bktc->bkfc/transpose | solution.py:77
  401.1 19.2 %bitcast_convert_fusion.1 = bf16[2048,128,32]{1,2,0:T(8,128)(2,1)} fusion(f32[8,2,2048,128]{3,0,1,2:T(8,128)} %copy.38, s32[8,2]{0,1:T(2,128)S(1)} %bitcast.81), kind=kOutput, calls=%fused_computation.4 | convolution fusion | flops 1619001856 | bytes 33554496 | tf_op jit(solution)/shard_map/bkj,bkfc->fjc/dot_general | solution.py:80
  420.2 0.0 copy-start.1
  420.2 17.3 %copy.52 = bf16[256,8,32,128]{3,1,2,0:T(8,128)(2,1)} copy(bf16[256,8,32,128]{3,2,1,0:T(8,128)(2,1)} %bitcast.67) | data formatting | bytes 33554432
  437.6 0.0 copy-done.1
  (4 shorter events, 0.0 us)
Async XLA Ops:
  7.2 88.0 %copy-start = (f32[4096]{0:T(1024)S(1)}, f32[4096]{0:T(1024)}, u32[]{:S(2)}) copy-start(f32[4096]{0:T(1024)} %param.9) | copy-start | bytes 49156
  7.2 113.4 %reduce-scatter.2.cloned.1.call-start = ((), (), s32[]{:S(2)}) async-start(), calls=%async_computation.1 | async-start | bytes 589824 | tf_op jit(solution)/shard_map/reduce_scatter | solution.py:33
  75.8 7.9 %copy-start.3 = (s32[8,1,2]{0,2,1:T(2,128)S(1)}, s32[8,1,2]{0,2,1:T(2,128)}, u32[]{:S(2)}) copy-start(s32[8,1,2]{0,2,1:T(2,128)} %param.12) | copy-start | bytes 196
  75.8 8.0 %copy-start.5 = (s32[8,1]{0,1:T(1,128)S(1)}, s32[8,1]{0,1:T(1,128)}, u32[]{:S(2)}) copy-start(s32[8,1]{0,1:T(1,128)} %param.13) | copy-start | bytes 100
  83.6 210.1 %all-reduce.3.cloned.1.call-start = ((), (), s32[]{:S(2)}) async-start(), calls=%async_computation.2 | async-start | bytes 8388608 | tf_op jit(solution)/shard_map/psum | solution.py:55
  131.6 162.1 %copy-start.4 = (f32[2048]{0:T(1024)S(1)}, f32[2048]{0:T(1024)}, u32[]{:S(2)}) copy-start(f32[2048]{0:T(1024)} %param.11) | copy-start | bytes 24580
  138.5 233.9 %all-reduce.5.cloned.1.call-start = ((), (), s32[]{:S(2)}) async-start(), calls=%async_computation.3 | async-start | bytes 1048576 | tf_op jit(solution)/shard_map/psum | solution.py:66
  299.2 2.0 copy-start.2
  420.2 17.3 %copy-start.1 = (f32[4096]{0:T(1024)S(1)}, f32[4096]{0:T(1024)}, u32[]{:S(2)}) copy-start(f32[4096]{0:T(1024)} %param.9) | copy-start | bytes 49156
Sparse Core Ops, SparseCore 0:
  83.7 36.8 reduce-scatter.1
  138.7 154.9 all-reduce.2
  318.6 53.7 all-reduce.4
where the time goes:
time: 446 us; the launch traced here: 444 us
  waiting for transfers between devices  185 us (41%)
  local copies, waits for them, and re-layouts  138 us (31%)
  matrix products  88.5 us (20%)
  between operations  13.8 us (3%)
  blocking collectives  9.81 us (2%)
  other arithmetic  8.61 us (2%)
    psum x1, waiting for transfers between devices, local(): lax.psum(partial_value.reshape(all_blocks * TB, features).astype(jnp.bflo...  155 us
    unnamed x14, local copies, waits for them, and re-layouts  41.8 us
    dot_general x1, matrix products, local(): jnp.einsum('bkj,bkcf->jcf', selector, tile_grads, precision=lax.Precision...  26.5 us
    reduce_scatter x1, waiting for transfers between devices, local(): lax.psum_scatter(jnp.einsum('btf,fbkc->bktc', block_rows, weight_tiles, p...  24.2 us
    reshape x1, local copies, waits for them, and re-layouts, local(): enc_cube = enc_weight.reshape(features, lat_blocks, LB)  22.4 us
    gather x2, local copies, waits for them, and re-layouts, local(): weight_tiles = jnp.take(enc_cube, chosen, axis=1)  22.1 us
    convert_element_type x1, local copies, waits for them, and re-layouts, local(): dec_grad = dec_total.reshape(lat_dev, features).astype(jnp.bfloat16)  20.9 us
    dot_general x1, matrix products, local(): jnp.einsum('bkj,bkfc->fjc', chosen, products, precision=lax.Precision.HIG...  19.2 us
  transfers between devices with their start and end apart: 3, of which 3 were waited for; matrix products, arithmetic and copies ran while one was open for 14% of the time, Pallas kernels for 0%

commit v1 on v0

v1 whole, which is shorter than its diff:
```python
import functools

import jax
import jax.numpy as jnp
from jax import lax
from jax.experimental import pallas as pl
from jax.experimental.pallas import tpu as pltpu
from jax.sharding import PartitionSpec as P

TB = 128
LB = 128
KS = 2

SCALE_ERR = 0.0625
PENALTY = 0.05
F32 = jnp.float32
BF16 = jnp.bfloat16
MESH = pl.DeviceIdType.MESH
VMEM = pltpu.VMEM
BIG = 60 * 1024 * 1024


def dot(a, b, ca, cb):
    return lax.dot_general(a, b, (((ca,), (cb,)), ((), ())), preferred_element_type=F32)


def pre_kernel(ids, counts, cap_ref, enc_ref, bias_ref, pre_ref, bsel_ref, live_ref):
    i = pl.program_id(0)
    pre_ref[...] = dot(cap_ref[...], enc_ref[...], 1, 0).astype(BF16)
    bsel_ref[...] = bias_ref[...]
    on = (lax.rem(i, KS) < counts[i // KS]).astype(F32)
    live_ref[...] = jnp.full(live_ref.shape, on, F32)


def partial_pre(ids, counts, captured, enc_weight, enc_bias):
    features = captured.shape[1]
    slots = ids.shape[0]
    row = pl.BlockSpec((1, 1, LB), lambda i, ids, counts: (i, 0, 0))
    return pl.pallas_call(
        pre_kernel,
        grid_spec=pltpu.PrefetchScalarGridSpec(
            num_scalar_prefetch=2,
            grid=(slots,),
            in_specs=[
                pl.BlockSpec((TB, features), lambda i, ids, counts: (i // KS, 0)),
                pl.BlockSpec((features, LB), lambda i, ids, counts: (0, ids[i])),
                pl.BlockSpec((1, 1, LB), lambda i, ids, counts: (ids[i], 0, 0)),
            ],
            out_specs=[pl.BlockSpec((TB, LB), lambda i, ids, counts: (i, 0)), row, row],
        ),
        out_shape=[
            jax.ShapeDtypeStruct((slots * TB, LB), BF16),
            jax.ShapeDtypeStruct((slots, 1, LB), F32),
            jax.ShapeDtypeStruct((slots, 1, LB), F32),
        ],
        compiler_params=pltpu.CompilerParams(vmem_limit_bytes=BIG),
        name="partial_pre",
    )(ids, counts, captured, enc_weight, enc_bias.reshape(-1, 1, LB))


def exchange_kernel(n, finish, part_ref, *refs):
    *extra, out_ref, recv, send_sem, recv_sem, give_sem, got_sem = refs
    me = lax.axis_index("tok")
    barrier = pltpu.get_barrier_semaphore()
    for d in range(1, n):
        pl.semaphore_signal(barrier, inc=1, device_id={"tok": lax.rem(me + d, n)}, device_id_type=MESH)
    pl.semaphore_wait(barrier, n - 1)
    outgoing = []
    for d in range(1, n):
        peer = lax.rem(me + d, n)
        copy = pltpu.make_async_remote_copy(
            src_ref=part_ref.at[peer],
            dst_ref=recv.at[d - 1],
            send_sem=send_sem.at[d - 1],
            recv_sem=recv_sem.at[d - 1],
            device_id={"tok": peer},
            device_id_type=MESH,
        )
        copy.start()
        outgoing.append(copy)
    for copy in outgoing:
        copy.wait()
    total = part_ref[me].astype(F32)
    for d in range(1, n):
        total = total + recv[d - 1].astype(F32)
    out_ref[me] = finish(me, total, *extra)
    outgoing = []
    for d in range(1, n):
        copy = pltpu.make_async_remote_copy(
            src_ref=out_ref.at[me],
            dst_ref=out_ref.at[me],
            send_sem=give_sem.at[d - 1],
            recv_sem=got_sem.at[d - 1],
            device_id={"tok": lax.rem(me + d, n)},
            device_id_type=MESH,
        )
        copy.start()
        outgoing.append(copy)
    for copy in outgoing:
        copy.wait_send()
    for d in range(1, n):
        source = lax.rem(me + n - d, n)
        pltpu.make_async_remote_copy(
            src_ref=out_ref.at[source],
            dst_ref=out_ref.at[source],
            send_sem=give_sem.at[d - 1],
            recv_sem=got_sem.at[d - 1],
            device_id={"tok": source},
            device_id_type=MESH,
        ).wait_recv()


def exchange(finish, ident, name, part, *extra):
    n = lax.axis_size("tok")
    rows = part.shape[0] // n
    whole = pl.BlockSpec(memory_space=VMEM)
    out = pl.pallas_call(
        functools.partial(exchange_kernel, n, finish),
        out_shape=jax.ShapeDtypeStruct((n, rows, LB), BF16),
        in_specs=[whole] * (1 + len(extra)),
        out_specs=whole,
        scratch_shapes=[VMEM((n - 1, rows, LB), BF16)] + [pltpu.SemaphoreType.DMA((n - 1,))] * 4,
        compiler_params=pltpu.CompilerParams(
            collective_id=ident, has_side_effects=True, vmem_limit_bytes=BIG
        ),
        name=name,
    )(part.reshape(n, rows, LB), *extra)
    return out.reshape(n * rows, LB)


def make_codes(me, total, bias_ref, live_ref):
    slots = total.shape[0] // TB
    outs = []
    for s in range(slots):
        v = total[s * TB:(s + 1) * TB] + bias_ref[me * slots + s]
        soft = jnp.maximum(v, 0.0) + jnp.log1p(jnp.exp(-jnp.abs(v)))
        outs.append((soft * live_ref[me * slots + s]).astype(BF16))
    return jnp.concatenate(outs, axis=0)


def make_dpre(me, total, codes_ref):
    return ((total + PENALTY) * (1.0 - jnp.exp(-codes_ref[me].astype(F32)))).astype(BF16)


def part_kernel(ids, codes_ref, *refs):
    *dec_refs, out_ref = refs
    total = dot(codes_ref[0:TB], dec_refs[0][...], 1, 0)
    for k in range(1, KS):
        total = total + dot(codes_ref[k * TB:(k + 1) * TB], dec_refs[k][...], 1, 0)
    out_ref[...] = total.astype(BF16)


def dec_specs(features):
    return [
        pl.BlockSpec((LB, features), functools.partial(lambda k, b, ids: (ids[b * KS + k], 0), k))
        for k in range(KS)
    ]


def rebuild_part(ids, codes, dec_weight):
    features = dec_weight.shape[1]
    blocks = ids.shape[0] // KS
    return pl.pallas_call(
        part_kernel,
        grid_spec=pltpu.PrefetchScalarGridSpec(
            num_scalar_prefetch=1,
            grid=(blocks,),
            in_specs=[pl.BlockSpec((KS * TB, LB), lambda b, ids: (b, 0))] + dec_specs(features),
            out_specs=pl.BlockSpec((TB, features), lambda b, ids: (b, 0)),
        ),
        out_shape=jax.ShapeDtypeStruct((blocks * TB, features), BF16),
        compiler_params=pltpu.CompilerParams(vmem_limit_bytes=BIG),
        name="rebuild_part",
    )(ids, codes, *([dec_weight] * KS))


def line_kernel(
    n, chunk, lag, part_ref, cap_ref, bias_ref, out_ref, up_in, down_in, up_out, down_out,
    up_send, up_recv, down_send, down_recv,
):
    me = lax.axis_index("lat")
    chunks = part_ref.shape[0] // chunk
    has_low = me > 0
    has_high = me < n - 1
    low = jnp.maximum(me - 1, 0)
    high = jnp.minimum(me + 1, n - 1)
    barrier = pltpu.get_barrier_semaphore()

    @pl.when(has_low)
    def _():
        pl.semaphore_signal(barrier, inc=1, device_id={"lat": low}, device_id_type=MESH)

    @pl.when(has_high)
    def _():
        pl.semaphore_signal(barrier, inc=1, device_id={"lat": high}, device_id_type=MESH)

    pl.semaphore_wait(barrier, has_low.astype(jnp.int32) + has_high.astype(jnp.int32))

    def rows(c):
        return pl.ds(pl.multiple_of(c * chunk, chunk), chunk)

    def up(c):
        return pltpu.make_async_remote_copy(
            src_ref=up_out.at[rows(c)], dst_ref=up_in.at[rows(c)],
            send_sem=up_send.at[c], recv_sem=up_recv.at[c],
            device_id={"lat": high}, device_id_type=MESH,
        )

    def up_first(c):
        return pltpu.make_async_remote_copy(
            src_ref=part_ref.at[rows(c)], dst_ref=up_in.at[rows(c)],
            send_sem=up_send.at[c], recv_sem=up_recv.at[c],
            device_id={"lat": high}, device_id_type=MESH,
        )

    def down(c):
        return pltpu.make_async_remote_copy(
            src_ref=down_out.at[rows(c)], dst_ref=down_in.at[rows(c)],
            send_sem=down_send.at[c], recv_sem=down_recv.at[c],
            device_id={"lat": low}, device_id_type=MESH,
        )

    def down_first(c):
        return pltpu.make_async_remote_copy(
            src_ref=part_ref.at[rows(c)], dst_ref=down_in.at[rows(c)],
            send_sem=down_send.at[c], recv_sem=down_recv.at[c],
            device_id={"lat": low}, device_id_type=MESH,
        )

    up_delay = lag * me
    down_delay = lag * (n - 1 - me)
    last_delay = jnp.maximum(up_delay, down_delay)

    def step(i, carry):
        cu = i - up_delay
        cd = i - down_delay
        cl = i - last_delay

        @pl.when(jnp.logical_and(cu >= 0, cu < chunks))
        def _():
            @pl.when(has_low)
            def _():
                up(cu).wait_recv()

                @pl.when(has_high)
                def _():
                    up_out[rows(cu)] = (up_in[rows(cu)].astype(F32) + part_ref[rows(cu)].astype(F32)).astype(BF16)
                    up(cu).start()

            @pl.when(jnp.logical_not(has_low))
            def _():
                up_first(cu).start()

        @pl.when(jnp.logical_and(cd >= 0, cd < chunks))
        def _():
            @pl.when(has_high)
            def _():
                down(cd).wait_recv()

                @pl.when(has_low)
                def _():
                    down_out[rows(cd)] = (down_in[rows(cd)].astype(F32) + part_ref[rows(cd)].astype(F32)).astype(BF16)
                    down(cd).start()

            @pl.when(jnp.logical_not(has_high))
            def _():
                down_first(cd).start()

        @pl.when(jnp.logical_and(cl >= 0, cl < chunks))
        def _():
            own = part_ref[rows(cl)].astype(F32) + bias_ref[...] - cap_ref[rows(cl)].astype(F32)

            @pl.when(jnp.logical_and(has_low, has_high))
            def _():
                both = up_in[rows(cl)].astype(F32) + down_in[rows(cl)].astype(F32)
                out_ref[rows(cl)] = (SCALE_ERR * (own + both)).astype(BF16)

            @pl.when(jnp.logical_not(has_low))
            def _():
                out_ref[rows(cl)] = (SCALE_ERR * (own + down_in[rows(cl)].astype(F32))).astype(BF16)

            @pl.when(jnp.logical_not(has_high))
            def _():
                out_ref[rows(cl)] = (SCALE_ERR * (own + up_in[rows(cl)].astype(F32))).astype(BF16)

        return carry

    lax.fori_loop(0, chunks + lag * (n - 1), step, 0)

    def drain(c, carry):
        @pl.when(has_high)
        def _():
            up(c).wait_send()

        @pl.when(has_low)
        def _():
            down(c).wait_send()

        return carry

    lax.fori_loop(0, chunks, drain, 0)


def line_delta(part, captured, dec_bias, chunk, lag):
    n = lax.axis_size("lat")
    tokens, features = part.shape
    chunks = tokens // chunk
    whole = pl.BlockSpec(memory_space=VMEM)
    return pl.pallas_call(
        functools.partial(line_kernel, n, chunk, lag),
        out_shape=jax.ShapeDtypeStruct((tokens, features), BF16),
        in_specs=[whole] * 3,
        out_specs=whole,
        scratch_shapes=[VMEM((tokens, features), BF16)] * 4 + [pltpu.SemaphoreType.DMA((chunks,))] * 4,
        compiler_params=pltpu.CompilerParams(
            collective_id=1, has_side_effects=True, vmem_limit_bytes=BIG
        ),
        name="line_delta",
    )(part, captured, dec_bias.reshape(1, features))


def dcodes_kernel(ids, delta_ref, *refs):
    *dec_refs, out_ref = refs
    for k in range(KS):
        out_ref[k * TB:(k + 1) * TB] = dot(delta_ref[...], dec_refs[k][...], 1, 1).astype(BF16)


def partial_dcodes(ids, delta, dec_weight):
    features = dec_weight.shape[1]
    blocks = ids.shape[0] // KS
    return pl.pallas_call(
        dcodes_kernel,
        grid_spec=pltpu.PrefetchScalarGridSpec(
            num_scalar_prefetch=1,
            grid=(blocks,),
            in_specs=[pl.BlockSpec((TB, features), lambda b, ids: (b, 0))] + dec_specs(features),
            out_specs=pl.BlockSpec((KS * TB, LB), lambda b, ids: (b, 0)),
        ),
        out_shape=jax.ShapeDtypeStruct((blocks * KS * TB, LB), BF16),
        compiler_params=pltpu.CompilerParams(vmem_limit_bytes=BIG),
        name="partial_dcodes",
    )(ids, delta, *([dec_weight] * KS))


def grads_kernel(slots, ids, delta_ref, codes_ref, cap_ref, dpre_ref, enc_ref, dec_ref, dec_acc, enc_acc):
    j = pl.program_id(0)

    def look(s, found):
        hit = ids[s] == j
        first = jnp.logical_and(hit, found == 0)
        again = jnp.logical_and(hit, found > 0)
        tokens = pl.ds(pl.multiple_of((s // KS) * TB, TB), TB)
        mine = pl.ds(pl.multiple_of(s * TB, TB), TB)

        def tiles():
            return (
                dot(codes_ref[mine], delta_ref[tokens], 0, 0),
                dot(cap_ref[tokens], dpre_ref[mine], 0, 0),
            )

        @pl.when(first)
        def _():
            dec_acc[...], enc_acc[...] = tiles()

        @pl.when(again)
        def _():
            d, e = tiles()
            dec_acc[...] += d
            enc_acc[...] += e

        return found + hit.astype(jnp.int32)

    found = lax.fori_loop(0, slots, look, jnp.int32(0))

    @pl.when(found > 0)
    def _():
        dec_ref[...] = dec_acc[...].astype(BF16)
        enc_ref[...] = enc_acc[...].astype(BF16)

    @pl.when(found == 0)
    def _():
        dec_ref[...] = jnp.zeros(dec_ref.shape, BF16)
        enc_ref[...] = jnp.zeros(enc_ref.shape, BF16)


def gradients(ids, delta, codes, captured, dpre, lat_dev):
    features = delta.shape[1]
    slots = ids.shape[0]
    whole = pl.BlockSpec(memory_space=VMEM)
    return pl.pallas_call(
        functools.partial(grads_kernel, slots),
        grid_spec=pltpu.PrefetchScalarGridSpec(
            num_scalar_prefetch=1,
            grid=(lat_dev // LB,),
            in_specs=[whole] * 4,
            out_specs=[
                pl.BlockSpec((features, LB), lambda j, ids: (0, j)),
                pl.BlockSpec((LB, features), lambda j, ids: (j, 0)),
            ],
            scratch_shapes=[VMEM((LB, features), F32), VMEM((features, LB), F32)],
        ),
        out_shape=[
            jax.ShapeDtypeStruct((features, lat_dev), BF16),
            jax.ShapeDtypeStruct((lat_dev, features), BF16),
        ],
        compiler_params=pltpu.CompilerParams(vmem_limit_bytes=BIG),
        name="gradients",
    )(ids, delta, codes, captured, dpre)


def local(captured, enc_weight, enc_bias, dec_weight, dec_bias, block_ids, block_counts):
    n = lax.axis_size("tok")
    ids = block_ids.reshape(-1)
    counts = block_counts.reshape(-1)
    pre, bias, live = partial_pre(ids, counts, captured, enc_weight, enc_bias)
    codes = exchange(make_codes, 0, "codes_exchange", pre, bias, live)
    part = rebuild_part(ids, codes, dec_weight)
    delta = line_delta(part, captured, dec_bias, 32, 2)
    dcodes = partial_dcodes(ids, delta, dec_weight)
    dpre = exchange(make_dpre, 2, "dpre_exchange", dcodes, codes.reshape(n, -1, LB))
    return tuple(gradients(ids, delta, codes, captured, dpre, enc_weight.shape[1]))


def solution(mesh):
    in_specs = (
        P(None, "tok"),
        P("tok", "lat"),
        P("lat"),
        P("lat", "tok"),
        P("tok"),
        P(None, "lat", None),
        P(None, "lat"),
    )
    out_specs = (P("tok", "lat"), P("lat", "tok"))
    return jax.shard_map(local, mesh=mesh, in_specs=in_specs, out_specs=out_specs, check_vma=False)
```

time: 446 us -> 216 us (0.48)
  Pallas kernels: 0 us -> 213 us
  waiting for transfers between devices: 185 us -> 0 us
  local copies, waits for them, and re-layouts: 138 us -> 1.41 us
  matrix products: 88.5 us -> 0 us
  between operations: 13.8 us -> 0.66 us
  blocking collectives: 9.81 us -> 0 us
  other arithmetic: 8.61 us -> 0 us
    pallas_call x0 -> x7, Pallas kernels: none -> 213 us  [the longest x1 112 us: line_delta(): pl.pallas_call(functools.partial(line_kernel, n, chunk, lag), out_shape=j...]
    psum x2 -> x0, waiting for transfers between devices: 161 us -> none  [the longest x1 155 us: local(): lax.psum(partial_value.reshape(all_blocks * TB, features).astype(jnp.bflo...]
    dot_general x7 -> x0, matrix products: 88.5 us -> none  [the longest x1 26.5 us: local(): jnp.einsum('bkj,bkcf->jcf', selector, tile_grads, precision=lax.Precision...]
    unnamed x14 -> x1, local copies, waits for them, and re-layouts: 41.8 us -> 0.75 us
    gather x4 -> x0, local copies, waits for them, and re-layouts: 33.3 us -> none  [the longest x2 22.1 us: local(): weight_tiles = jnp.take(enc_cube, chosen, axis=1)]
    reduce_scatter x1 -> x0, waiting for transfers between devices: 24.2 us -> none  [local(): lax.psum_scatter(jnp.einsum('btf,fbkc->bktc', block_rows, weight_tiles, p...]
    reshape x1, local copies, waits for them, and re-layouts: 22.4 us -> 0.66 us  [local(): ids = block_ids.reshape(-1)]
    convert_element_type x2 -> x0, local copies, waits for them, and re-layouts: 21.1 us -> none  [the longest x1 20.9 us: local(): dec_grad = dec_total.reshape(lat_dev, features).astype(jnp.bfloat16)]
  transfers between devices with their start and end apart: 3 -> 0, of which waited for: 3 -> 0; matrix products, arithmetic and copies ran while one was open for 14% -> 0% of each run, Pallas kernels for 0% -> 0%
where the time goes in v1:
time: 216 us; the launch traced here: 215 us
  Pallas kernels  213 us (99%)
    pallas_call x1, Pallas kernels, line_delta(): pl.pallas_call(functools.partial(line_kernel, n, chunk, lag), out_shape=j...  112 us
    pallas_call x2, Pallas kernels, exchange(): pl.pallas_call(functools.partial(exchange_kernel, n, finish), out_shape=j...  38 us
    pallas_call x1, Pallas kernels, gradients(): pl.pallas_call(functools.partial(grads_kernel, slots), grid_spec=pltpu.Pr...  30.3 us
    pallas_call x1, Pallas kernels, partial_pre(): pl.pallas_call(pre_kernel, grid_spec=pltpu.PrefetchScalarGridSpec(num_sca...  14.2 us
    pallas_call x1, Pallas kernels, partial_dcodes(): pl.pallas_call(dcodes_kernel, grid_spec=pltpu.PrefetchScalarGridSpec(num_...  9.55 us
    pallas_call x1, Pallas kernels, rebuild_part(): pl.pallas_call(part_kernel, grid_spec=pltpu.PrefetchScalarGridSpec(num_sc...  9.54 us

profile of v1, /device:TPU:0, one launch (start us, length us, event | category | flops | bytes accessed | tf_op | source)
XLA Modules:
  0.0 215.2 jit_solution(13043213832248711409)
XLA Ops:
  0.6 0.8 copy.10
  1.4 0.7 reshape.28.ids
  2.0 14.2 %partial_pre.1 = (bf16[2048,128]{1,0:T(8,128)(2,1)}, f32[16,1,128]{2,1,0:T(1,128)}, f32[16,1,128]{2,1,0:T(1,128)}) custom-call(s32[16]{0:T(128)} %reshape.28.ids, s32[8]{0:T(128)} %bitcast.16, bf16[1024,2048]{1,0:T(8,128)(2,1)} %cap_ref.5, bf16[2048,4096]{1,0:T(8,128)(2,1)} %enc_ref.1, f32[32,1,128]{2,1,0:T(1,128)} %bitcast.14), custom_call_target="tpu_custom_call" | custom-call | tf_op jit(solution)/shard_map/partial_pre/pallas_call | solution.py:39
  16.2 19.8 %codes_exchange.1.refs_0_ = bf16[8,256,128]{2,1,0:T(8,128)(2,1)} custom-call(bf16[8,256,128]{2,1,0:T(8,128)(2,1)} %bitcast.13, f32[16,1,128]{2,1,0:T(1,128)} %get-tuple-element.6.refs_0_, f32[16,1,128]{2,1,0:T(1,128)} %get-tuple-element.7.refs_1_), custom_call_target="tpu_custom_call" | custom-call | tf_op jit(solution)/shard_map/codes_exchange/pallas_call | solution.py:117
  36.0 9.5 %rebuild_part.1.part_ref = bf16[1024,2048]{1,0:T(8,128)(2,1)} custom-call(s32[16]{0:T(128)} %reshape.28.ids, bf16[2048,128]{1,0:T(8,128)(2,1)} %bitcast.9, bf16[4096,2048]{1,0:T(8,128)(2,1)} %refs_1_.3, bf16[4096,2048]{1,0:T(8,128)(2,1)} %refs_1_.3), custom_call_target="tpu_custom_call" | custom-call | tf_op jit(solution)/shard_map/rebuild_part/pallas_call | solution.py:163
  45.5 111.6 %line_delta.1.delta_ref = bf16[1024,2048]{1,0:T(8,128)(2,1)} custom-call(bf16[1024,2048]{1,0:T(8,128)(2,1)} %rebuild_part.1.part_ref, bf16[1024,2048]{1,0:T(8,128)(2,1)} %cap_ref.5, f32[1,2048]{1,0:T(1,128)} %bitcast.15), custom_call_target="tpu_custom_call" | custom-call | tf_op jit(solution)/shard_map/line_delta/pallas_call | solution.py:309
  157.1 9.6 %partial_dcodes.1 = bf16[2048,128]{1,0:T(8,128)(2,1)} custom-call(s32[16]{0:T(128)} %reshape.28.ids, bf16[1024,2048]{1,0:T(8,128)(2,1)} %line_delta.1.delta_ref, bf16[4096,2048]{1,0:T(8,128)(2,1)} %refs_1_.3, bf16[4096,2048]{1,0:T(8,128)(2,1)} %refs_1_.3), custom_call_target="tpu_custom_call" | custom-call | tf_op jit(solution)/shard_map/partial_dcodes/pallas_call | solution.py:331
  166.7 18.3 %dpre_exchange.1 = bf16[8,256,128]{2,1,0:T(8,128)(2,1)} custom-call(bf16[8,256,128]{2,1,0:T(8,128)(2,1)} %bitcast.11, bf16[8,256,128]{2,1,0:T(8,128)(2,1)} %codes_exchange.1.refs_0_), custom_call_target="tpu_custom_call" | custom-call | tf_op jit(solution)/shard_map/dpre_exchange/pallas_call | solution.py:117
  185.0 30.3 %gradients.1 = (bf16[2048,4096]{1,0:T(8,128)(2,1)}, bf16[4096,2048]{1,0:T(8,128)(2,1)}) custom-call(s32[16]{0:T(128)} %reshape.28.ids, bf16[1024,2048]{1,0:T(8,128)(2,1)} %line_delta.1.delta_ref, bf16[2048,128]{1,0:T(8,128)(2,1)} %bitcast.10, bf16[1024,2048]{1,0:T(8,128)(2,1)} %cap_ref.5, bf16[2048,128]{1,0:T(8,128)(2,1)} %bitcast.12), custom_call_target="tpu_custom_call" | custom-call | tf_op jit(solution)/shard_map/gradients/pallas_call | solution.py:390

commit v2 on v0

v2 whole, which is shorter than its diff:
```python
import functools

import jax
import jax.numpy as jnp
from jax import lax
from jax.experimental import pallas as pl
from jax.experimental.pallas import tpu as pltpu
from jax.sharding import PartitionSpec as P

TB = 128
LB = 128
KS = 2

SCALE_ERR = 0.0625
PENALTY = 0.05
F32 = jnp.float32
BF16 = jnp.bfloat16
MESH = pl.DeviceIdType.MESH
VMEM = pltpu.VMEM
BIG = 60 * 1024 * 1024


def dot(a, b, ca, cb):
    return lax.dot_general(a, b, (((ca,), (cb,)), ((), ())), preferred_element_type=F32)


def pre_kernel(ids, counts, cap_ref, *refs):
    enc_refs, bias_refs, dec_refs = refs[:KS], refs[KS:2 * KS], refs[2 * KS:3 * KS]
    pre_ref, bsel_ref, live_ref, pack_ref = refs[3 * KS:]
    b = pl.program_id(0)
    tiles = jnp.concatenate([r[...] for r in enc_refs], axis=1)
    pre = dot(cap_ref[...], tiles, 1, 0).astype(BF16)
    for k in range(KS):
        pre_ref[k * TB:(k + 1) * TB] = pre[:, k * LB:(k + 1) * LB]
        bsel_ref[k] = bias_refs[k][0]
        live_ref[k] = jnp.full((1, LB), (k < counts[b]).astype(F32), F32)
        pack_ref[k * LB:(k + 1) * LB] = dec_refs[k][...]


def named(k, place):
    return lambda b, ids, counts: place(ids[b * KS + k])


def partial_pre(ids, counts, captured, enc_weight, enc_bias, dec_weight):
    features = captured.shape[1]
    slots = ids.shape[0]
    step = lambda b, ids, counts: (b, 0)
    row = pl.BlockSpec((KS, 1, LB), lambda b, ids, counts: (b, 0, 0))
    return pl.pallas_call(
        pre_kernel,
        grid_spec=pltpu.PrefetchScalarGridSpec(
            num_scalar_prefetch=2,
            grid=(slots // KS,),
            in_specs=[pl.BlockSpec((TB, features), step)]
            + [pl.BlockSpec((features, LB), named(k, lambda g: (0, g))) for k in range(KS)]
            + [pl.BlockSpec((1, 1, LB), named(k, lambda g: (g, 0, 0))) for k in range(KS)]
            + [pl.BlockSpec((LB, features), named(k, lambda g: (g, 0))) for k in range(KS)],
            out_specs=[
                pl.BlockSpec((KS * TB, LB), step), row, row, pl.BlockSpec((KS * LB, features), step),
            ],
        ),
        out_shape=[
            jax.ShapeDtypeStruct((slots * TB, LB), BF16),
            jax.ShapeDtypeStruct((slots, 1, LB), F32),
            jax.ShapeDtypeStruct((slots, 1, LB), F32),
            jax.ShapeDtypeStruct((slots * LB, features), BF16),
        ],
        compiler_params=pltpu.CompilerParams(vmem_limit_bytes=BIG),
        name="partial_pre",
    )(
        ids, counts, captured, *([enc_weight] * KS), *([enc_bias.reshape(-1, 1, LB)] * KS),
        *([dec_weight] * KS),
    )


def middle_kernel(
    n, nz, chunk, lag,
    pre_ref, bias_ref, live_ref, dbias_ref, cap_hbm, dec_hbm,
    codes_ref, dpre_ref, delta_hbm,
    cap_v, dec_v, part_v, delta_v, up_in, down_in, up_out, down_out,
    pre_in, dc_out, dc_in,
    up_send, up_recv, down_send, down_recv,
    pre_send, pre_recv, code_send, code_recv, dc_send, dc_recv, dp_send, dp_recv,
    load_sem, store_sem,
):
    me = lax.axis_index("tok")
    z = lax.axis_index("lat")
    group = part_v.shape[0] // n
    per = group // chunk
    own = group // TB
    chunks = n * per
    has_low = z > 0
    has_high = z < nz - 1
    inner = jnp.logical_and(has_low, has_high)
    low = jnp.maximum(z - 1, 0)
    high = jnp.minimum(z + 1, nz - 1)

    load_dec = pltpu.make_async_copy(dec_hbm, dec_v, load_sem.at[0])
    load_cap = pltpu.make_async_copy(cap_hbm, cap_v, load_sem.at[1])
    load_dec.start()
    load_cap.start()

    barrier = pltpu.get_barrier_semaphore()
    for d in range(1, n):
        pl.semaphore_signal(barrier, inc=1, device_id={"tok": lax.rem(me + d, n)}, device_id_type=MESH)

    @pl.when(has_low)
    def _():
        pl.semaphore_signal(barrier, inc=1, device_id={"lat": low}, device_id_type=MESH)

    @pl.when(has_high)
    def _():
        pl.semaphore_signal(barrier, inc=1, device_id={"lat": high}, device_id_type=MESH)

    pl.semaphore_wait(barrier, n - 1 + has_low.astype(jnp.int32) + has_high.astype(jnp.int32))

    def tok_copy(src, dst, send, recv, d, peer):
        return pltpu.make_async_remote_copy(
            src_ref=src, dst_ref=dst, send_sem=send.at[d - 1], recv_sem=recv.at[d - 1],
            device_id={"tok": peer}, device_id_type=MESH,
        )

    outgoing = []
    for d in range(1, n):
        peer = lax.rem(me + d, n)
        copy = tok_copy(pre_ref.at[peer], pre_in.at[d - 1], pre_send, pre_recv, d, peer)
        copy.start()
        outgoing.append(copy)
    for copy in outgoing:
        copy.wait()
    total = pre_ref[me].astype(F32)
    for d in range(1, n):
        total = total + pre_in[d - 1].astype(F32)
    outs = []
    for s in range(own * KS):
        v = total[s * TB:(s + 1) * TB] + bias_ref[me * own * KS + s]
        soft = jnp.maximum(v, 0.0) + jnp.log1p(jnp.exp(-jnp.abs(v)))
        outs.append((soft * live_ref[me * own * KS + s]).astype(BF16))
    codes_ref[me] = jnp.concatenate(outs, axis=0)

    def give_codes(d):
        return tok_copy(codes_ref.at[me], codes_ref.at[me], code_send, code_recv, d, lax.rem(me + n - d, n))

    def get_codes(d, g):
        return tok_copy(codes_ref.at[g], codes_ref.at[g], code_send, code_recv, d, lax.rem(me + n - d, n))

    for d in range(1, n):
        give_codes(d).start()
    load_dec.wait()
    load_cap.wait()

    def group_of(i):
        return lax.rem(me + i, n)

    def rows(c):
        return pl.ds(pl.multiple_of(group_of(c // per) * group + lax.rem(c, per) * chunk, chunk), chunk)

    def line_copy(src, dst, send, recv, c, dev):
        return pltpu.make_async_remote_copy(
            src_ref=src.at[rows(c)], dst_ref=dst.at[rows(c)], send_sem=send.at[c], recv_sem=recv.at[c],
            device_id={"lat": dev}, device_id_type=MESH,
        )

    def up(c):
        return line_copy(up_out, up_in, up_send, up_recv, c, high)

    def up_first(c):
        return line_copy(part_v, up_in, up_send, up_recv, c, high)

    def down(c):
        return line_copy(down_out, down_in, down_send, down_recv, c, low)

    def down_first(c):
        return line_copy(part_v, down_in, down_send, down_recv, c, low)

    def block_rows(g, o, size):
        return pl.ds(pl.multiple_of((g * own + o) * size, size), size)

    def make_part(g):
        for o in range(own):
            tiles = [codes_ref[g, pl.ds((o * KS + k) * TB, TB)] for k in range(KS)]
            value = dot(jnp.concatenate(tiles, axis=1), dec_v[block_rows(g, o, KS * LB)], 1, 0)
            part_v[block_rows(g, o, TB)] = value.astype(BF16)

    def delta_copy(g):
        span = pl.ds(pl.multiple_of(g * group, group), group)
        return pltpu.make_async_copy(delta_v.at[span], delta_hbm.at[span], store_sem.at[g])

    def give_dcodes(i):
        g = group_of(i)
        return tok_copy(dc_out.at[g], dc_in.at[i - 1], dc_send, dc_recv, i, g)

    up_delay = lag * z
    down_delay = lag * (nz - 1 - z)
    first_delay = jnp.minimum(up_delay, down_delay)
    last_delay = jnp.maximum(up_delay, down_delay)

    def step(t, carry):
        cf = t - first_delay
        cu = t - up_delay
        cd = t - down_delay
        cl = t - last_delay
        stage = jnp.maximum(cf, 0) // per

        @pl.when(jnp.logical_and(jnp.logical_and(cf >= 0, cf < chunks), lax.rem(jnp.maximum(cf, 0), per) == 0))
        def _():
            @pl.when(stage > 0)
            def _():
                get_codes(stage, group_of(stage)).wait_recv()

            make_part(group_of(stage))

        @pl.when(jnp.logical_and(cu >= 0, cu < chunks))
        def _():
            @pl.when(has_low)
            def _():
                up(cu).wait_recv()

                @pl.when(has_high)
                def _():
                    up_out[rows(cu)] = (up_in[rows(cu)].astype(F32) + part_v[rows(cu)].astype(F32)).astype(BF16)
                    up(cu).start()

            @pl.when(jnp.logical_not(has_low))
            def _():
                up_first(cu).start()

        @pl.when(jnp.logical_and(cd >= 0, cd < chunks))
        def _():
            @pl.when(has_high)
            def _():
                down(cd).wait_recv()

                @pl.when(has_low)
                def _():
                    down_out[rows(cd)] = (down_in[rows(cd)].astype(F32) + part_v[rows(cd)].astype(F32)).astype(BF16)
                    down(cd).start()

            @pl.when(jnp.logical_not(has_high))
            def _():
                down_first(cd).start()

        @pl.when(jnp.logical_and(cl >= 0, cl < chunks))
        def _():
            here = part_v[rows(cl)].astype(F32) + dbias_ref[...] - cap_v[rows(cl)].astype(F32)

            @pl.when(inner)
            def _():
                both = up_in[rows(cl)].astype(F32) + down_in[rows(cl)].astype(F32)
                delta_v[rows(cl)] = (SCALE_ERR * (here + both)).astype(BF16)

            @pl.when(jnp.logical_not(has_low))
            def _():
                delta_v[rows(cl)] = (SCALE_ERR * (here + down_in[rows(cl)].astype(F32))).astype(BF16)

            @pl.when(jnp.logical_not(has_high))
            def _():
                delta_v[rows(cl)] = (SCALE_ERR * (here + up_in[rows(cl)].astype(F32))).astype(BF16)

            done = cl // per

            @pl.when(lax.rem(cl, per) == per - 1)
            def _():
                g = group_of(done)
                for o in range(own):
                    value = dot(delta_v[block_rows(g, o, TB)], dec_v[block_rows(g, o, KS * LB)], 1, 1).astype(BF16)
                    for k in range(KS):
                        dc_out[g, pl.ds((o * KS + k) * TB, TB)] = value[:, k * LB:(k + 1) * LB]

                @pl.when(done > 0)
                def _():
                    give_dcodes(done).start()

                delta_copy(g).start()

        return carry

    lax.fori_loop(0, chunks + lag * (nz - 1), step, 0)

    total = dc_out[me].astype(F32)
    for d in range(1, n):
        give_dcodes(d).wait_recv()
        total = total + dc_in[d - 1].astype(F32)
    dpre_ref[me] = ((total + PENALTY) * (1.0 - jnp.exp(-codes_ref[me].astype(F32)))).astype(BF16)

    def give_dpre(d, g):
        return tok_copy(dpre_ref.at[g], dpre_ref.at[g], dp_send, dp_recv, d, lax.rem(me + n - d, n))

    for d in range(1, n):
        give_dpre(d, me).start()

    def drain(c, carry):
        @pl.when(has_high)
        def _():
            up(c).wait_send()

        @pl.when(has_low)
        def _():
            down(c).wait_send()

        return carry

    lax.fori_loop(0, chunks, drain, 0)
    for g in range(n):
        delta_copy(g).wait()
    for d in range(1, n):
        give_codes(d).wait_send()
        give_dcodes(d).wait_send()
        give_dpre(d, me).wait_send()
        give_dpre(d, group_of(d)).wait_recv()


def middle(pre, bias, live, dec_bias, captured, pack, chunk, lag):
    n = lax.axis_size("tok")
    nz = lax.axis_size("lat")
    tokens, features = captured.shape
    rows = pre.shape[0] // n
    chunks = tokens // chunk
    whole = pl.BlockSpec(memory_space=VMEM)
    outside = pl.BlockSpec(memory_space=pltpu.HBM)
    sems = lambda count: [pltpu.SemaphoreType.DMA((count,))]
    wide = VMEM((tokens, features), BF16)
    return pl.pallas_call(
        functools.partial(middle_kernel, n, nz, chunk, lag),
        out_shape=[
            jax.ShapeDtypeStruct((n, rows, LB), BF16),
            jax.ShapeDtypeStruct((n, rows, LB), BF16),
            jax.ShapeDtypeStruct((tokens, features), BF16),
        ],
        in_specs=[whole] * 4 + [outside] * 2,
        out_specs=[whole, whole, outside],
        scratch_shapes=[wide, VMEM(pack.shape, BF16)] + [wide] * 6
        + [VMEM((n - 1, rows, LB), BF16), VMEM((n, rows, LB), BF16), VMEM((n - 1, rows, LB), BF16)]
        + sems(chunks) * 4 + sems(n - 1) * 8 + sems(2) + sems(n),
        compiler_params=pltpu.CompilerParams(
            collective_id=0, has_side_effects=True, vmem_limit_bytes=BIG
        ),
        name="middle",
    )(pre.reshape(n, rows, LB), bias, live, dec_bias.reshape(1, features), captured, pack)


def grads_kernel(slots, ids, delta_ref, codes_ref, cap_ref, dpre_ref, enc_ref, dec_ref, dec_acc, enc_acc, head, after):
    j = pl.program_id(0)

    @pl.when(j == 0)
    def _():
        def clear(g, carry):
            head[g] = -1
            return carry

        lax.fori_loop(0, pl.num_programs(0), clear, 0)
        for s in reversed(range(slots)):
            after[s] = head[ids[s]]
            head[ids[s]] = s

    def tiles(s):
        tokens = pl.ds(pl.multiple_of((s // KS) * TB, TB), TB)
        mine = pl.ds(pl.multiple_of(s * TB, TB), TB)
        return (
            dot(codes_ref[mine], delta_ref[tokens], 0, 0),
            dot(cap_ref[tokens], dpre_ref[mine], 0, 0),
        )

    start = head[j]

    @pl.when(start < 0)
    def _():
        dec_ref[...] = jnp.zeros(dec_ref.shape, BF16)
        enc_ref[...] = jnp.zeros(enc_ref.shape, BF16)

    @pl.when(start >= 0)
    def _():
        more = after[start]

        @pl.when(more < 0)
        def _():
            d, e = tiles(start)
            dec_ref[...] = d.astype(BF16)
            enc_ref[...] = e.astype(BF16)

        @pl.when(more >= 0)
        def _():
            dec_acc[...], enc_acc[...] = tiles(start)

            def add(s):
                d, e = tiles(s)
                dec_acc[...] += d
                enc_acc[...] += e
                return after[s]

            lax.while_loop(lambda s: s >= 0, add, more)
            dec_ref[...] = dec_acc[...].astype(BF16)
            enc_ref[...] = enc_acc[...].astype(BF16)


def gradients(ids, delta, codes, captured, dpre, lat_dev):
    features = delta.shape[1]
    slots = ids.shape[0]
    whole = pl.BlockSpec(memory_space=VMEM)
    return pl.pallas_call(
        functools.partial(grads_kernel, slots),
        grid_spec=pltpu.PrefetchScalarGridSpec(
            num_scalar_prefetch=1,
            grid=(lat_dev // LB,),
            in_specs=[whole] * 4,
            out_specs=[
                pl.BlockSpec((features, LB), lambda j, ids: (0, j)),
                pl.BlockSpec((LB, features), lambda j, ids: (j, 0)),
            ],
            scratch_shapes=[
                VMEM((LB, features), F32), VMEM((features, LB), F32),
                pltpu.SMEM((lat_dev // LB,), jnp.int32), pltpu.SMEM((slots,), jnp.int32),
            ],
        ),
        out_shape=[
            jax.ShapeDtypeStruct((features, lat_dev), BF16),
            jax.ShapeDtypeStruct((lat_dev, features), BF16),
        ],
        compiler_params=pltpu.CompilerParams(vmem_limit_bytes=BIG),
        name="gradients",
    )(ids, delta, codes, captured, dpre)


def local(captured, enc_weight, enc_bias, dec_weight, dec_bias, block_ids, block_counts):
    ids = block_ids.reshape(-1)
    counts = block_counts.reshape(-1)
    pre, bias, live, pack = partial_pre(ids, counts, captured, enc_weight, enc_bias, dec_weight)
    codes, dpre, delta = middle(pre, bias, live, dec_bias, captured, pack, 16, 4)
    codes, dpre = codes.reshape(-1, LB), dpre.reshape(-1, LB)
    return tuple(gradients(ids, delta, codes, captured, dpre, enc_weight.shape[1]))


def solution(mesh):
    in_specs = (
        P(None, "tok"),
        P("tok", "lat"),
        P("lat"),
        P("lat", "tok"),
        P("tok"),
        P(None, "lat", None),
        P(None, "lat"),
    )
    out_specs = (P("tok", "lat"), P("lat", "tok"))
    return jax.shard_map(local, mesh=mesh, in_specs=in_specs, out_specs=out_specs, check_vma=False)
```

time: 446 us -> 169 us (0.38)
  waiting for transfers between devices: 185 us -> 0 us
  Pallas kernels: 0 us -> 167 us
  local copies, waits for them, and re-layouts: 138 us -> 1.38 us
  matrix products: 88.5 us -> 0 us
  between operations: 13.8 us -> 0.64 us
  blocking collectives: 9.81 us -> 0 us
  other arithmetic: 8.61 us -> 0 us
    pallas_call x0 -> x3, Pallas kernels: none -> 167 us  [the longest x1 128 us: middle(): pl.pallas_call(functools.partial(middle_kernel, n, nz, chunk, lag), out_s...]
    psum x2 -> x0, waiting for transfers between devices: 161 us -> none  [the longest x1 155 us: local(): lax.psum(partial_value.reshape(all_blocks * TB, features).astype(jnp.bflo...]
    dot_general x7 -> x0, matrix products: 88.5 us -> none  [the longest x1 26.5 us: local(): jnp.einsum('bkj,bkcf->jcf', selector, tile_grads, precision=lax.Precision...]
    unnamed x14 -> x1, local copies, waits for them, and re-layouts: 41.8 us -> 0.75 us
    gather x4 -> x0, local copies, waits for them, and re-layouts: 33.3 us -> none  [the longest x2 22.1 us: local(): weight_tiles = jnp.take(enc_cube, chosen, axis=1)]
    reduce_scatter x1 -> x0, waiting for transfers between devices: 24.2 us -> none  [local(): lax.psum_scatter(jnp.einsum('btf,fbkc->bktc', block_rows, weight_tiles, p...]
    reshape x1, local copies, waits for them, and re-layouts: 22.4 us -> 0.62 us  [local(): ids = block_ids.reshape(-1)]
    convert_element_type x2 -> x0, local copies, waits for them, and re-layouts: 21.1 us -> none  [the longest x1 20.9 us: local(): dec_grad = dec_total.reshape(lat_dev, features).astype(jnp.bfloat16)]
  transfers between devices with their start and end apart: 3 -> 0, of which waited for: 3 -> 0; matrix products, arithmetic and copies ran while one was open for 14% -> 0% of each run, Pallas kernels for 0% -> 0%
where the time goes in v2:
time: 169 us
  Pallas kernels  167 us (99%)
    pallas_call x1, Pallas kernels, middle(): pl.pallas_call(functools.partial(middle_kernel, n, nz, chunk, lag), out_s...  128 us
    pallas_call x1, Pallas kernels, gradients(): pl.pallas_call(functools.partial(grads_kernel, slots), grid_spec=pltpu.Pr...  26 us
    pallas_call x1, Pallas kernels, partial_pre(): pl.pallas_call(pre_kernel, grid_spec=pltpu.PrefetchScalarGridSpec(num_sca...  13.3 us

profile of v2, /device:TPU:0, one launch (start us, length us, event | category | flops | bytes accessed | tf_op | source)
XLA Modules:
  0.0 169.2 jit_solution(4491506740985997262)
XLA Ops:
  0.6 0.8 copy.10
  1.4 0.6 reshape.25.ids
  2.0 13.3 %partial_pre.1 = (bf16[2048,128]{1,0:T(8,128)(2,1)}, f32[16,1,128]{2,1,0:T(1,128)}, f32[16,1,128]{2,1,0:T(1,128)}, bf16[2048,2048]{1,0:T(8,128)(2,1)}) custom-call(s32[16]{0:T(128)} %reshape.25.ids, s32[8]{0:T(128)} %bitcast.14, bf16[1024,2048]{1,0:T(8,128)(2,1)} %cap_ref.3, bf16[2048,4096]{1,0:T(8,128)(2,1)} %refs_1_.1, bf16[2048,4096]{1,0:T(8,128)(2,1)} %refs_1_.1, ...), custom_call_target="tpu_custom_call" | custom-call | tf_op jit(solution)/shard_map/partial_pre/pallas_call | solution.py:49
  15.3 128.0 %middle.1 = (bf16[8,256,128]{2,1,0:T(8,128)(2,1)}, bf16[8,256,128]{2,1,0:T(8,128)(2,1)}, bf16[1024,2048]{1,0:T(8,128)(2,1)}) custom-call(bf16[8,256,128]{2,1,0:T(8,128)(2,1)} %bitcast.10, f32[16,1,128]{2,1,0:T(1,128)} %get-tuple-element.10.bias_ref, f32[16,1,128]{2,1,0:T(1,128)} %get-tuple-element.11.live_ref, f32[1,2048]{1,0:T(1,128)} %bitcast.13, ...), custom_call_target="tpu_custom_call" | custom-call | tf_op jit(solution)/shard_map/middle/pallas_call | solution.py:323
  143.3 26.0 %gradients.1 = (bf16[2048,4096]{1,0:T(8,128)(2,1)}, bf16[4096,2048]{1,0:T(8,128)(2,1)}) custom-call(s32[16]{0:T(128)} %reshape.25.ids, bf16[1024,2048]{1,0:T(8,128)(2,1)} %get-tuple-element.13.delta_ref, bf16[2048,128]{1,0:T(8,128)(2,1)} %bitcast.8, bf16[1024,2048]{1,0:T(8,128)(2,1)} %cap_ref.3, bf16[2048,128]{1,0:T(8,128)(2,1)} %bitcast.9), custom_call_target="tpu_custom_call" | custom-call | tf_op jit(solution)/shard_map/gradients/pallas_call | solution.py:400

commit v3 on v2

--- a/solution.py
+++ b/solution.py
@@ -25,25 +25,69 @@
 
 
 def pre_kernel(ids, counts, cap_ref, *refs):
-    enc_refs, bias_refs, dec_refs = refs[:KS], refs[KS:2 * KS], refs[2 * KS:3 * KS]
-    pre_ref, bsel_ref, live_ref, pack_ref = refs[3 * KS:]
+    enc_refs, bias_refs = refs[:KS], refs[KS:2 * KS]
+    pre_ref, bsel_ref, live_ref, order_ref, tile_ref, first_ref, place = refs[2 * KS:]
     b = pl.program_id(0)
+
+    @pl.when(b == 0)
+    def _():
+        def clear(g, carry):
+            place[g] = 0
+            return carry
+
+        def count(s, carry):
+            place[ids[s]] += 1
+            return carry
+
+        def unnamed(g, at):
+            @pl.when(place[g] == 0)
+            def _():
+                tile_ref[at] = g
+
+            return at + (place[g] == 0).astype(jnp.int32)
+
+        def taken(g, at):
+            @pl.when(place[g] > 0)
+            def _():
+                tile_ref[at] = g
+
+            return at + (place[g] > 0).astype(jnp.int32)
+
+        def offset(g, seen):
+            here = place[g]
+            place[g] = seen
+            first_ref[g] = seen
+            return seen + here
+
+        def put(s, carry):
+            at = place[ids[s]]
+            order_ref[at] = s
+            place[ids[s]] = at + 1
+            return carry
+
+        slots, groups = order_ref.shape[0], place.shape[0]
+        lax.fori_loop(0, groups, clear, 0)
+        lax.fori_loop(0, slots, count, 0)
+        lax.fori_loop(0, groups, taken, lax.fori_loop(0, groups, unnamed, jnp.int32(0)))
+        first_ref[groups] = lax.fori_loop(0, groups, offset, jnp.int32(0))
+        lax.fori_loop(0, slots, put, 0)
+
     tiles = jnp.concatenate([r[...] for r in enc_refs], axis=1)
     pre = dot(cap_ref[...], tiles, 1, 0).astype(BF16)
     for k in range(KS):
         pre_ref[k * TB:(k + 1) * TB] = pre[:, k * LB:(k + 1) * LB]
         bsel_ref[k] = bias_refs[k][0]
         live_ref[k] = jnp.full((1, LB), (k < counts[b]).astype(F32), F32)
-        pack_ref[k * LB:(k + 1) * LB] = dec_refs[k][...]
 
 
 def named(k, place):
     return lambda b, ids, counts: place(ids[b * KS + k])
 
 
-def partial_pre(ids, counts, captured, enc_weight, enc_bias, dec_weight):
+def partial_pre(ids, counts, captured, enc_weight, enc_bias):
     features = captured.shape[1]
     slots = ids.shape[0]
+    groups = enc_weight.shape[1] // LB
     step = lambda b, ids, counts: (b, 0)
     row = pl.BlockSpec((KS, 1, LB), lambda b, ids, counts: (b, 0, 0))
     return pl.pallas_call(
@@ -53,29 +97,30 @@
             grid=(slots // KS,),
             in_specs=[pl.BlockSpec((TB, features), step)]
             + [pl.BlockSpec((features, LB), named(k, lambda g: (0, g))) for k in range(KS)]
-            + [pl.BlockSpec((1, 1, LB), named(k, lambda g: (g, 0, 0))) for k in range(KS)]
-            + [pl.BlockSpec((LB, features), named(k, lambda g: (g, 0))) for k in range(KS)],
+            + [pl.BlockSpec((1, 1, LB), named(k, lambda g: (g, 0, 0))) for k in range(KS)],
             out_specs=[
-                pl.BlockSpec((KS * TB, LB), step), row, row, pl.BlockSpec((KS * LB, features), step),
-            ],
+                pl.BlockSpec((KS * TB, LB), step), row, row,
+            ] + [pl.BlockSpec(memory_space=pltpu.SMEM)] * 3,
+            scratch_shapes=[pltpu.SMEM((groups,), jnp.int32)],
         ),
         out_shape=[
             jax.ShapeDtypeStruct((slots * TB, LB), BF16),
             jax.ShapeDtypeStruct((slots, 1, LB), F32),
             jax.ShapeDtypeStruct((slots, 1, LB), F32),
-            jax.ShapeDtypeStruct((slots * LB, features), BF16),
+            jax.ShapeDtypeStruct((slots,), jnp.int32),
+            jax.ShapeDtypeStruct((groups,), jnp.int32),
+            jax.ShapeDtypeStruct((groups + 1,), jnp.int32),
         ],
         compiler_params=pltpu.CompilerParams(vmem_limit_bytes=BIG),
         name="partial_pre",
     )(
         ids, counts, captured, *([enc_weight] * KS), *([enc_bias.reshape(-1, 1, LB)] * KS),
-        *([dec_weight] * KS),
     )
 
 
 def middle_kernel(
     n, nz, chunk, lag,
-    pre_ref, bias_ref, live_ref, dbias_ref, cap_hbm, dec_hbm,
+    ids, pre_ref, bias_ref, live_ref, dbias_ref, cap_hbm, dec_hbm,
     codes_ref, dpre_ref, delta_hbm,
     cap_v, dec_v, part_v, delta_v, up_in, down_in, up_out, down_out,
     pre_in, dc_out, dc_in,
@@ -176,10 +221,14 @@
     def block_rows(g, o, size):
         return pl.ds(pl.multiple_of((g * own + o) * size, size), size)
 
+    def dec_tile(g, o):
+        first = (g * own + o) * KS
+        return jnp.concatenate([dec_v[ids[first + k]] for k in range(KS)], axis=0)
+
     def make_part(g):
         for o in range(own):
             tiles = [codes_ref[g, pl.ds((o * KS + k) * TB, TB)] for k in range(KS)]
-            value = dot(jnp.concatenate(tiles, axis=1), dec_v[block_rows(g, o, KS * LB)], 1, 0)
+            value = dot(jnp.concatenate(tiles, axis=1), dec_tile(g, o), 1, 0)
             part_v[block_rows(g, o, TB)] = value.astype(BF16)
 
     def delta_copy(g):
@@ -263,7 +312,7 @@
             def _():
                 g = group_of(done)
                 for o in range(own):
-                    value = dot(delta_v[block_rows(g, o, TB)], dec_v[block_rows(g, o, KS * LB)], 1, 1).astype(BF16)
+                    value = dot(delta_v[block_rows(g, o, TB)], dec_tile(g, o), 1, 1).astype(BF16)
                     for k in range(KS):
                         dc_out[g, pl.ds((o * KS + k) * TB, TB)] = value[:, k * LB:(k + 1) * LB]
 
@@ -310,11 +359,12 @@
         give_dpre(d, group_of(d)).wait_recv()
 
 
-def middle(pre, bias, live, dec_bias, captured, pack, chunk, lag):
+def middle(ids, pre, bias, live, dec_bias, captured, dec_weight, chunk, lag):
     n = lax.axis_size("tok")
     nz = lax.axis_size("lat")
     tokens, features = captured.shape
     rows = pre.shape[0] // n
+    lat_dev = dec_weight.shape[0]
     chunks = tokens // chunk
     whole = pl.BlockSpec(memory_space=VMEM)
     outside = pl.BlockSpec(memory_space=pltpu.HBM)
@@ -327,107 +377,138 @@
             jax.ShapeDtypeStruct((n, rows, LB), BF16),
             jax.ShapeDtypeStruct((tokens, features), BF16),
         ],
-        in_specs=[whole] * 4 + [outside] * 2,
+        in_specs=[pl.BlockSpec(memory_space=pltpu.SMEM)] + [whole] * 4 + [outside] * 2,
         out_specs=[whole, whole, outside],
-        scratch_shapes=[wide, VMEM(pack.shape, BF16)] + [wide] * 6
+        scratch_shapes=[wide, VMEM((lat_dev // LB, LB, features), BF16)] + [wide] * 6
         + [VMEM((n - 1, rows, LB), BF16), VMEM((n, rows, LB), BF16), VMEM((n - 1, rows, LB), BF16)]
         + sems(chunks) * 4 + sems(n - 1) * 8 + sems(2) + sems(n),
         compiler_params=pltpu.CompilerParams(
             collective_id=0, has_side_effects=True, vmem_limit_bytes=BIG
         ),
         name="middle",
-    )(pre.reshape(n, rows, LB), bias, live, dec_bias.reshape(1, features), captured, pack)
-
-
-def grads_kernel(slots, ids, delta_ref, codes_ref, cap_ref, dpre_ref, enc_ref, dec_ref, dec_acc, enc_acc, head, after):
-    j = pl.program_id(0)
-
-    @pl.when(j == 0)
-    def _():
-        def clear(g, carry):
-            head[g] = -1
+    )(
+        ids, pre.reshape(n, rows, LB), bias, live, dec_bias.reshape(1, features), captured,
+        dec_weight.reshape(-1, LB, features),
+    )
+
+
+def grads_kernel(
+    order, tile, first, delta_hbm, codes_ref, cap_hbm, dpre_ref,
+    enc_ref, dec_ref, delta_v, cap_v, dec_acc, enc_acc, state, delta_sem, cap_sem,
+):
+    i = pl.program_id(0)
+    start = first[tile[i]]
+    stop = first[tile[i] + 1]
+
+    def loads(b):
+        span = pl.ds(pl.multiple_of(b * TB, TB), TB)
+        return (
+            pltpu.make_async_copy(delta_hbm.at[span], delta_v.at[span], delta_sem.at[b]),
+            pltpu.make_async_copy(cap_hbm.at[span], cap_v.at[span], cap_sem.at[b]),
+        )
+
+    @pl.when(i == 0)
+    def _():
+        def clear(b, carry):
+            state[b] = 0
             return carry
 
-        lax.fori_loop(0, pl.num_programs(0), clear, 0)
-        for s in reversed(range(slots)):
-            after[s] = head[ids[s]]
-            head[ids[s]] = s
-
-    def tiles(s):
-        tokens = pl.ds(pl.multiple_of((s // KS) * TB, TB), TB)
+        def begin(t, carry):
+            b = order[t] // KS
+
+            @pl.when(state[b] == 0)
+            def _():
+                for copy in loads(b):
+                    copy.start()
+                state[b] = 1
+
+            return carry
+
+        lax.fori_loop(0, state.shape[0], clear, 0)
+        lax.fori_loop(0, order.shape[0], begin, 0)
+
+    def tiles(t):
+        s = order[t]
+        b = s // KS
+
+        @pl.when(state[b] == 1)
+        def _():
+            for copy in loads(b):
+                copy.wait()
+            state[b] = 2
+
+        tokens = pl.ds(pl.multiple_of(b * TB, TB), TB)
         mine = pl.ds(pl.multiple_of(s * TB, TB), TB)
         return (
-            dot(codes_ref[mine], delta_ref[tokens], 0, 0),
-            dot(cap_ref[tokens], dpre_ref[mine], 0, 0),
+            dot(codes_ref[mine], delta_v[tokens], 0, 0),
+            dot(cap_v[tokens], dpre_ref[mine], 0, 0),
         )
 
-    start = head[j]
-
-    @pl.when(start < 0)
+    @pl.when(stop == start)
     def _():
         dec_ref[...] = jnp.zeros(dec_ref.shape, BF16)
         enc_ref[...] = jnp.zeros(enc_ref.shape, BF16)
 
-    @pl.when(start >= 0)
-    def _():
-        more = after[start]
-
-        @pl.when(more < 0)
-        def _():
-            d, e = tiles(start)
-            dec_ref[...] = d.astype(BF16)
-            enc_ref[...] = e.astype(BF16)
-
-        @pl.when(more >= 0)
-        def _():
-            dec_acc[...], enc_acc[...] = tiles(start)
-
-            def add(s):
-                d, e = tiles(s)
-                dec_acc[...] += d
-                enc_acc[...] += e
-                return after[s]
-
-            lax.while_loop(lambda s: s >= 0, add, more)
-            dec_ref[...] = dec_acc[...].astype(BF16)
-            enc_ref[...] = enc_acc[...].astype(BF16)
-
-
-def gradients(ids, delta, codes, captured, dpre, lat_dev):
-    features = delta.shape[1]
-    slots = ids.shape[0]
+    @pl.when(stop == start + 1)
+    def _():
+        d, e = tiles(start)
+        dec_ref[...] = d.astype(BF16)
+        enc_ref[...] = e.astype(BF16)
+
+    @pl.when(stop > start + 1)
+    def _():
+        dec_acc[...], enc_acc[...] = tiles(start)
+
+        def add(t, carry):
+            d, e = tiles(t)
+            dec_acc[...] += d
+            enc_acc[...] += e
+            return carry
+
+        lax.fori_loop(start + 1, stop, add, 0)
+        dec_ref[...] = dec_acc[...].astype(BF16)
+        enc_ref[...] = enc_acc[...].astype(BF16)
+
+
+def gradients(order, tile, first, delta, codes, captured, dpre):
+    tokens, features = delta.shape
+    blocks = tokens // TB
+    groups = tile.shape[0]
     whole = pl.BlockSpec(memory_space=VMEM)
+    outside = pl.BlockSpec(memory_space=pltpu.HBM)
     return pl.pallas_call(
-        functools.partial(grads_kernel, slots),
+        grads_kernel,
         grid_spec=pltpu.PrefetchScalarGridSpec(
-            num_scalar_prefetch=1,
-            grid=(lat_dev // LB,),
-            in_specs=[whole] * 4,
+            num_scalar_prefetch=3,
+            grid=(groups,),
+            in_specs=[outside, whole, outside, whole],
             out_specs=[
-                pl.BlockSpec((features, LB), lambda j, ids: (0, j)),
-                pl.BlockSpec((LB, features), lambda j, ids: (j, 0)),
+                pl.BlockSpec((features, LB), lambda i, order, tile, first: (0, tile[i])),
+                pl.BlockSpec((LB, features), lambda i, order, tile, first: (tile[i], 0)),
             ],
             scratch_shapes=[
+                VMEM((tokens, features), BF16), VMEM((tokens, features), BF16),
                 VMEM((LB, features), F32), VMEM((features, LB), F32),
-                pltpu.SMEM((lat_dev // LB,), jnp.int32), pltpu.SMEM((slots,), jnp.int32),
+                pltpu.SMEM((blocks,), jnp.int32),
+                pltpu.SemaphoreType.DMA((blocks,)), pltpu.SemaphoreType.DMA((blocks,)),
             ],
         ),
         out_shape=[
-            jax.ShapeDtypeStruct((features, lat_dev), BF16),
-            jax.ShapeDtypeStruct((lat_dev, features), BF16),
+            jax.ShapeDtypeStruct((features, groups * LB), BF16),
+            jax.ShapeDtypeStruct((groups * LB, features), BF16),
         ],
         compiler_params=pltpu.CompilerParams(vmem_limit_bytes=BIG),
         name="gradients",
-    )(ids, delta, codes, captured, dpre)
+    )(order, tile, first, delta, codes, captured, dpre)
 
 
 def local(captured, enc_weight, enc_bias, dec_weight, dec_bias, block_ids, block_counts):
     ids = block_ids.reshape(-1)
     counts = block_counts.reshape(-1)
-    pre, bias, live, pack = partial_pre(ids, counts, captured, enc_weight, enc_bias, dec_weight)
-    codes, dpre, delta = middle(pre, bias, live, dec_bias, captured, pack, 16, 4)
+    pre, bias, live, order, tile, first = partial_pre(ids, counts, captured, enc_weight, enc_bias)
+    codes, dpre, delta = middle(ids, pre, bias, live, dec_bias, captured, dec_weight, 16, 4)
     codes, dpre = codes.reshape(-1, LB), dpre.reshape(-1, LB)
-    return tuple(gradients(ids, delta, codes, captured, dpre, enc_weight.shape[1]))
+    return tuple(gradients(order, tile, first, delta, codes, captured, dpre))
 
 
 def solution(mesh):

time: 169 us -> 163 us (0.964)
  Pallas kernels: 167 us -> 161 us
    pallas_call x1, Pallas kernels: 13.3 us -> 9.33 us  [partial_pre(): pl.pallas_call(pre_kernel, grid_spec=pltpu.PrefetchScalarGridSpec(num_sca...]
    pallas_call x1, Pallas kernels: 26 us -> 23.4 us  [gradients(): pl.pallas_call(grads_kernel, grid_spec=pltpu.PrefetchScalarGridSpec(num_s...]
where the time goes in v3:
time: 163 us
  Pallas kernels  161 us (99%)
    pallas_call x1, Pallas kernels, middle(): pl.pallas_call(functools.partial(middle_kernel, n, nz, chunk, lag), out_s...  128 us
    pallas_call x1, Pallas kernels, gradients(): pl.pallas_call(grads_kernel, grid_spec=pltpu.PrefetchScalarGridSpec(num_s...  23.4 us
    pallas_call x1, Pallas kernels, partial_pre(): pl.pallas_call(pre_kernel, grid_spec=pltpu.PrefetchScalarGridSpec(num_sca...  9.33 us

profile of v3, /device:TPU:0, one launch (start us, length us, event | category | flops | bytes accessed | tf_op | source)
XLA Modules:
  0.0 162.7 jit_solution(726061317776186951)
XLA Ops:
  0.6 0.8 copy.10
  1.4 0.6 reshape.28.ids
  2.0 9.3 %partial_pre.1 = (bf16[2048,128]{1,0:T(8,128)(2,1)}, f32[16,1,128]{2,1,0:T(1,128)}, f32[16,1,128]{2,1,0:T(1,128)}, s32[16]{0:T(128)}, s32[32]{0:T(128)}, /*index=5*/s32[33]{0:T(128)}) custom-call(s32[16]{0:T(128)} %reshape.28.ids, s32[8]{0:T(128)} %bitcast.16, bf16[1024,2048]{1,0:T(8,128)(2,1)} %cap_hbm.3, bf16[2048,4096]{1,0:T(8,128)(2,1)} %refs_1_.1, ...), custom_call_target="tpu_custom_call" | custom-call | tf_op jit(solution)/shard_map/partial_pre/pallas_call | solution.py:93
  11.3 128.0 %middle.1 = (bf16[8,256,128]{2,1,0:T(8,128)(2,1)}, bf16[8,256,128]{2,1,0:T(8,128)(2,1)}, bf16[1024,2048]{1,0:T(8,128)(2,1)}) custom-call(s32[16]{0:T(128)} %reshape.28.ids, bf16[8,256,128]{2,1,0:T(8,128)(2,1)} %bitcast.12, f32[16,1,128]{2,1,0:T(1,128)} %get-tuple-element.15.bias_ref, f32[16,1,128]{2,1,0:T(1,128)} %get-tuple-element.16.live_ref, ...), custom_call_target="tpu_custom_call" | custom-call | tf_op jit(solution)/shard_map/middle/pallas_call | solution.py:373
  139.3 23.4 %gradients.1 = (bf16[2048,4096]{1,0:T(8,128)(2,1)}, bf16[4096,2048]{1,0:T(8,128)(2,1)}) custom-call(s32[16]{0:T(128)} %get-tuple-element.11.order, s32[32]{0:T(128)} %get-tuple-element.12.tile, s32[33]{0:T(128)} %get-tuple-element.13.first, bf16[1024,2048]{1,0:T(8,128)(2,1)} %get-tuple-element.17.delta_hbm, bf16[2048,128]{1,0:T(8,128)(2,1)} %bitcast.10, ...), custom_call_target="tpu_custom_call" | custom-call | tf_op jit(solution)/shard_map/gradients/pallas_call | solution.py:479

commit v4 on v3

--- a/solution.py
+++ b/solution.py
@@ -39,19 +39,16 @@
             place[ids[s]] += 1
             return carry
 
-        def unnamed(g, at):
-            @pl.when(place[g] == 0)
-            def _():
-                tile_ref[at] = g
-
-            return at + (place[g] == 0).astype(jnp.int32)
-
-        def taken(g, at):
-            @pl.when(place[g] > 0)
-            def _():
-                tile_ref[at] = g
-
-            return at + (place[g] > 0).astype(jnp.int32)
+        def free(g, seen):
+            return seen + (place[g] == 0).astype(jnp.int32)
+
+        def visit(g, seen):
+            named_one = place[g] > 0
+            taken = g - seen
+            late = jnp.where(taken < pairs, lead + 2 * taken + 1, unnamed + taken)
+            early = jnp.where(seen < lead, seen, 2 * seen - lead)
+            tile_ref[jnp.where(named_one, late, early)] = g
+            return seen + 1 - named_one.astype(jnp.int32)
 
         def offset(g, seen):
             here = place[g]
@@ -68,7 +65,10 @@
         slots, groups = order_ref.shape[0], place.shape[0]
         lax.fori_loop(0, groups, clear, 0)
         lax.fori_loop(0, slots, count, 0)
-        lax.fori_loop(0, groups, taken, lax.fori_loop(0, groups, unnamed, jnp.int32(0)))
+        unnamed = lax.fori_loop(0, groups, free, jnp.int32(0))
+        lead = jnp.maximum(2 * unnamed - groups, 0)
+        pairs = unnamed - lead
+        lax.fori_loop(0, groups, visit, jnp.int32(0))
         first_ref[groups] = lax.fori_loop(0, groups, offset, jnp.int32(0))
         lax.fori_loop(0, slots, put, 0)
 

time: 163 us -> 165 us (1.012)
  Pallas kernels: 161 us -> 163 us
    pallas_call x1, Pallas kernels: 23.4 us -> 25.8 us  [gradients(): pl.pallas_call(grads_kernel, grid_spec=pltpu.PrefetchScalarGridSpec(num_s...]
where the time goes in v4:
time: 165 us
  Pallas kernels  163 us (99%)
    pallas_call x1, Pallas kernels, middle(): pl.pallas_call(functools.partial(middle_kernel, n, nz, chunk, lag), out_s...  128 us
    pallas_call x1, Pallas kernels, gradients(): pl.pallas_call(grads_kernel, grid_spec=pltpu.PrefetchScalarGridSpec(num_s...  25.8 us
    pallas_call x1, Pallas kernels, partial_pre(): pl.pallas_call(pre_kernel, grid_spec=pltpu.PrefetchScalarGridSpec(num_sca...  9.25 us

profile of v4, /device:TPU:0, one launch (start us, length us, event | category | flops | bytes accessed | tf_op | source)
XLA Modules:
  0.0 165.1 jit_solution(26210460691278101)
XLA Ops:
  0.6 0.8 copy.10
  1.4 0.6 reshape.28.ids
  2.0 9.2 %partial_pre.1 = (bf16[2048,128]{1,0:T(8,128)(2,1)}, f32[16,1,128]{2,1,0:T(1,128)}, f32[16,1,128]{2,1,0:T(1,128)}, s32[16]{0:T(128)}, s32[32]{0:T(128)}, /*index=5*/s32[33]{0:T(128)}) custom-call(s32[16]{0:T(128)} %reshape.28.ids, s32[8]{0:T(128)} %bitcast.16, bf16[1024,2048]{1,0:T(8,128)(2,1)} %cap_hbm.3, bf16[2048,4096]{1,0:T(8,128)(2,1)} %refs_1_.1, ...), custom_call_target="tpu_custom_call" | custom-call | tf_op jit(solution)/shard_map/partial_pre/pallas_call | solution.py:93
  11.2 128.1 %middle.1 = (bf16[8,256,128]{2,1,0:T(8,128)(2,1)}, bf16[8,256,128]{2,1,0:T(8,128)(2,1)}, bf16[1024,2048]{1,0:T(8,128)(2,1)}) custom-call(s32[16]{0:T(128)} %reshape.28.ids, bf16[8,256,128]{2,1,0:T(8,128)(2,1)} %bitcast.12, f32[16,1,128]{2,1,0:T(1,128)} %get-tuple-element.15.bias_ref, f32[16,1,128]{2,1,0:T(1,128)} %get-tuple-element.16.live_ref, ...), custom_call_target="tpu_custom_call" | custom-call | tf_op jit(solution)/shard_map/middle/pallas_call | solution.py:373
  139.3 25.8 %gradients.1 = (bf16[2048,4096]{1,0:T(8,128)(2,1)}, bf16[4096,2048]{1,0:T(8,128)(2,1)}) custom-call(s32[16]{0:T(128)} %get-tuple-element.11.order, s32[32]{0:T(128)} %get-tuple-element.12.tile, s32[33]{0:T(128)} %get-tuple-element.13.first, bf16[1024,2048]{1,0:T(8,128)(2,1)} %get-tuple-element.17.delta_hbm, bf16[2048,128]{1,0:T(8,128)(2,1)} %bitcast.10, ...), custom_call_target="tpu_custom_call" | custom-call | tf_op jit(solution)/shard_map/gradients/pallas_call | solution.py:479
